TPU v7x, 32 devices: a whole 2x2x4 slice. The times are simulated.
32 devices in a mesh: row: 4 (over y, x), col: 8 (over z, core).
Axes of the slice: x: 2, y: 2, z: 4, core: 2. Of those that a mesh axis runs over, the one named last changes fastest.
Arguments:
- vectors: float32 [4608, 4096], P('row', 'col'), may hold values from -6 to 6
- reflectors: float32 [256, 2304], P('col', 'row'), may hold values from -0.75 to 0.75
Outputs:
- result: float32 [4608, 4096], P('row', 'col')
All inputs are finite; a program needn't handle non-finite values.
Results may differ from a plain program's by a relative error of at most 0.00019.
Values sent between devices are 32-bit elements; how exact they have to be, the bound alone decides.
A program may use at most 64 MiB of HBM per device.

v0:
```python
import functools

import jax
import jax.numpy as jnp
from jax import lax
from jax.experimental import pallas as pl
from jax.experimental.pallas import tpu as pltpu
from jax.sharding import PartitionSpec as P

BAND = 64
GROUPS = 4
WIN = 2 * BAND
HALO = GROUPS * BAND
SIDE = GROUPS // 2


def group_range(group, own):
    return group // 2, own + GROUPS - group


def split(x):
    high = x.astype(jnp.bfloat16)
    low = (x - high.astype(jnp.float32)).astype(jnp.bfloat16)
    return high, low


def dot(a, b, dims=(1, 0)):
    return lax.dot_general(
        a, b, (((dims[0],), (dims[1],)), ((), ())), preferred_element_type=jnp.float32
    )


def product(a, b):
    ah, al = split(a)
    bh, bl = split(b)
    return dot(jnp.concatenate([ah, al], 1), jnp.concatenate([bh, bh], 0)) + dot(ah, bl)


def prep_kernel(own, all_windows, refl_ref, q_ref):
    group = pl.program_id(0)
    first = lax.axis_index("row") * own - SIDE
    size = WIN
    held = own + 2 * SIDE
    pairs = (held + 1) // 2
    row = lax.broadcasted_iota(jnp.int32, (size, size), 0)
    lane = lax.broadcasted_iota(jnp.int32, (size, size), 1)
    eye = row == lane
    identity = eye.astype(jnp.float32)
    upper = (row // BAND == lane // BAND) & (row < lane)
    inside = (row // BAND) == (lane // BAND)
    lead = inside & (lane % BAND == 0)

    skews, nils, invs, scaled = [], [], [], []
    for pair in range(pairs):
        if (pair + 1) * size <= held * BAND:
            slab = refl_ref[:, pair * size : (pair + 1) * size]
        else:
            part = refl_ref[:, pair * size : pair * size + BAND]
            slab = jnp.concatenate([part, jnp.zeros_like(part)], 1)
        both = jnp.concatenate([slab, slab], 0)
        both = jnp.where(lead, 1.0, jnp.where(inside, both, 0.0))
        skews.append(pltpu.roll(both, 0, 1, stride=1, stride_axis=0))
    for pair in range(pairs):
        high, low = split(skews[pair])
        gram = dot(
            jnp.concatenate([high, low], 1), jnp.concatenate([high, high], 1), (1, 1)
        ) + dot(high, low, (1, 1))
        diag = 0.5 * jnp.sum(jnp.where(eye, gram, 0.0), axis=1, keepdims=True)
        scale = 1.0 / diag
        nils.append(jnp.where(upper, gram * scale, 0.0))
        scaled.append(skews[pair] * scale)
    block = BAND // 4
    near = row // block == lane // block
    powers = [jnp.where(near, n, 0.0) for n in nils]
    invs = [identity - p for p in powers]
    powers = [product(p, p) for p in powers]
    for level in range(2):
        stacked = [product(jnp.concatenate([i, p], 0), p) for i, p in zip(invs, powers)]
        invs = [i + s[:size] for i, s in zip(invs, stacked)]
        powers = [s[size:] for s in stacked]
    invs = [i + product(i, p) for i, p in zip(invs, powers)]
    for _ in range(2):
        wide = row // (2 * block) == lane // (2 * block)
        far = wide & (row // block != lane // block)
        cross = [product(jnp.where(far, n, 0.0), i) for n, i in zip(nils, invs)]
        invs = [i - product(i, c) for i, c in zip(invs, cross)]
        block *= 2
    solved = [product(i, s) for i, s in zip(invs, scaled)]
    usable = all_windows - group % 2
    for pair in range(pairs):
        sh, sl = split(skews[pair])
        th, tl = split(solved[pair])
        for half in range(2):
            k = 2 * pair + half
            if k >= held:
                continue
            at = slice(half * BAND, (half + 1) * BAND)
            left = jnp.concatenate([sh[at], sl[at], sh[at]], 0)
            right = jnp.concatenate([th[at], th[at], tl[at]], 0)
            change = dot(left, right, (0, 0))
            window = first + k
            weight = ((window >= 0) & (window < usable)).astype(jnp.float32)
            high, low = split(identity - weight * change)
            q_ref[0, k, :, :size] = high
            q_ref[0, k, :, size:] = low


def apply_kernel(own, q_ref, above_ref, x_ref, below_ref, out_ref, work_ref):
    rows = x_ref.shape[0]
    for group in range(GROUPS):
        start, count = group_range(group, own)
        for k in range(start, start + count):
            at = BAND * (group % 2) + WIN * k
            if group == 0:
                if at < HALO:
                    block = above_ref[at : at + WIN, :]
                elif at < HALO + rows:
                    block = x_ref[at - HALO : at - HALO + WIN, :]
                else:
                    block = below_ref[at - HALO - rows : at - HALO - rows + WIN, :]
            else:
                block = work_ref[at : at + WIN, :]
            xh, xl = split(block)
            q = q_ref[group, k]
            new = dot(q, jnp.concatenate([xh, xh], 0)) + dot(q[:, :WIN], xl)
            if group < GROUPS - 1:
                work_ref[at : at + WIN, :] = new
            else:
                low, high = max(at, HALO), min(at + WIN, HALO + rows)
                out_ref[low - HALO : high - HALO, :] = new[low - at : high - at, :]


def shards(vectors, reflectors):
    rows, columns = vectors.shape
    own = rows // WIN
    count = lax.axis_size("row")
    forward = [(i, i + 1) for i in range(count - 1)]
    backward = [(i + 1, i) for i in range(count - 1)]
    width = SIDE * BAND
    before = lax.ppermute(reflectors[:, reflectors.shape[1] - width :], "row", forward)
    after = lax.ppermute(reflectors[:, :width], "row", backward)
    above = lax.ppermute(vectors[rows - HALO :], "row", forward)
    below = lax.ppermute(vectors[:HALO], "row", backward)
    stored = jnp.concatenate([before, reflectors, after], 1)
    everything = lax.all_gather(stored, "col", axis=0, tiled=True)

    held = own + 2 * SIDE
    q = pl.pallas_call(
        functools.partial(prep_kernel, own, own * count),
        grid=(GROUPS,),
        in_specs=[pl.BlockSpec((BAND, held * BAND), lambda g: (g, 0))],
        out_specs=pl.BlockSpec((1, held, WIN, 2 * WIN), lambda g: (g, 0, 0, 0)),
        out_shape=jax.ShapeDtypeStruct((GROUPS, held, WIN, 2 * WIN), jnp.bfloat16),
        cost_estimate=pl.CostEstimate(
            flops=GROUPS * held * 60 * WIN**3, bytes_accessed=2**22, transcendentals=0
        ),
        name="prep",
    )(everything)
    tile = min(columns, 256)
    return pl.pallas_call(
        functools.partial(apply_kernel, own),
        grid=(columns // tile,),
        in_specs=[
            pl.BlockSpec(q.shape, lambda c: (0, 0, 0, 0)),
            pl.BlockSpec((HALO, tile), lambda c: (0, c)),
            pl.BlockSpec((rows, tile), lambda c: (0, c)),
            pl.BlockSpec((HALO, tile), lambda c: (0, c)),
        ],
        out_specs=pl.BlockSpec((rows, tile), lambda c: (0, c)),
        out_shape=jax.ShapeDtypeStruct(vectors.shape, vectors.dtype),
        scratch_shapes=[pltpu.VMEM((rows + 2 * HALO, tile), jnp.float32)],
        name="apply",
    )(q, above, vectors, below)


def solution(mesh):
    placed = (P("row", "col"), P("col", "row"))
    return jax.shard_map(
        shards, mesh=mesh, in_specs=placed, out_specs=P("row", "col"), check_vma=False
    )
```

profile of v0, /device:TPU:0, one launch (start us, length us, event | category | flops | bytes accessed | tf_op | source)
XLA Modules:
  0.0 55.3 jit_solution(16671016621473047325)
XLA Ops:
  0.0 0.8 %fusion.1 = (f32[32,128]{1,0:T(8,128)S(1)}, f32[32,128]{1,0:T(8,128)S(1)}) fusion(f32[32,576]{1,0:T(8,128)} %param.3), kind=kLoop, calls=%fused_computation.2 | loop fusion | bytes 65536 | tf_op jit(solution)/shard_map/slice | solution.py:140
  0.8 4.9 %collective-permute-start = (f32[32,128]{1,0:T(8,128)S(1)}, f32[32,128]{1,0:T(8,128)S(1)}, u32[]{:S(2)}, u32[]{:S(2)}) collective-permute-start(f32[32,128]{1,0:T(8,128)S(1)} %get-tuple-element.7), channel_id=1, source_target_pairs={{0,8},{8,16},{16,24},{1,9},{9,17},{17,25},{2,10},{10,18},{18,26},{... | collective-permute-start | bytes 49160 | tf_op jit(solution)/shard_map/ppermute | solution.py:140
  5.7 1.3 %collective-permute-start.1 = (f32[32,128]{1,0:T(8,128)S(1)}, f32[32,128]{1,0:T(8,128)S(1)}, u32[]{:S(2)}, u32[]{:S(2)}) collective-permute-start(f32[32,128]{1,0:T(8,128)S(1)} %get-tuple-element.8), channel_id=1, source_target_pairs={{8,0},{16,8},{24,16},{9,1},{17,9},{25,17},{10,2},{18,10},{26,18},{... | collective-permute-start | bytes 49160 | tf_op jit(solution)/shard_map/ppermute | solution.py:141
  7.0 1.3 %fusion = (f32[256,512]{1,0:T(8,128)S(1)}, f32[256,512]{1,0:T(8,128)S(1)}) fusion(f32[1152,512]{1,0:T(8,128)} %x_ref.1), kind=kLoop, calls=%fused_computation.1 | loop fusion | bytes 2097152 | tf_op jit(solution)/shard_map/slice | solution.py:143
  8.3 1.3 %collective-permute-start.3 = (f32[256,512]{1,0:T(8,128)S(1)}, f32[256,512]{1,0:T(8,128)S(1)}, u32[]{:S(2)}, u32[]{:S(2)}) collective-permute-start(f32[256,512]{1,0:T(8,128)S(1)} %get-tuple-element.5), channel_id=1, source_target_pairs={{8,0},{16,8},{24,16},{9,1},{17,9},{25,17},{10,2},{18,10},{26,18},{... | collective-permute-start | bytes 1572872 | tf_op jit(solution)/shard_map/ppermute | solution.py:143
  9.6 5.2 %collective-permute-start.2 = (f32[256,512]{1,0:T(8,128)S(1)}, f32[256,512]{1,0:T(8,128)S(1)}, u32[]{:S(2)}, u32[]{:S(2)}) collective-permute-start(f32[256,512]{1,0:T(8,128)S(1)} %get-tuple-element.6), channel_id=1, source_target_pairs={{0,8},{8,16},{16,24},{1,9},{9,17},{17,25},{2,10},{10,18},{18,26},{... | collective-permute-start | bytes 1572872 | tf_op jit(solution)/shard_map/ppermute | solution.py:142
  14.8 0.0 collective-permute-done
  14.8 0.0 collective-permute-done.1
  14.8 1.0 %pad_maximum_fusion = f32[32,832]{1,0:T(8,128)S(1)} fusion(f32[32,128]{1,0:T(8,128)S(1)} %collective-permute-done.1, f32[32,576]{1,0:T(8,128)} %param.3, f32[32,128]{1,0:T(8,128)S(1)} %collective-permute-done), kind=kLoop, calls=%fused_computation | loop fusion | flops 53248 | bytes 212992 | tf_op jit(solution)/shard_map/concatenate | solution.py:144
  15.8 17.3 %all_gather.3.refl_ref = f32[256,832]{1,0:T(8,128)} all-gather(f32[32,832]{1,0:T(8,128)S(1)} %pad_maximum_fusion), channel_id=1, replica_groups=mesh['row'=4,'col'=8] {'col'}, dimensions={0}, use_global_device_ids=true | all-gather | bytes 958464 | tf_op jit(solution)/shard_map/all_gather | solution.py:145
  33.0 13.2 %prep.1.q_ref = bf16[4,13,128,256]{3,2,1,0:T(8,128)(2,1)} custom-call(f32[256,832]{1,0:T(8,128)} %all_gather.3.refl_ref), custom_call_target="tpu_custom_call" | custom-call | flops 6543114240 | bytes 4194304 | tf_op jit(solution)/shard_map/prep/pallas_call | solution.py:148
  46.3 0.0 collective-permute-done.3.below_ref
  46.3 0.0 copy-start
  46.3 0.0 collective-permute-done.2.above_ref
  46.3 0.8 %copy-done = f32[256,512]{1,0:T(8,128)} copy-done((f32[256,512]{1,0:T(8,128)}, f32[256,512]{1,0:T(8,128)S(1)}, u32[]{:S(2)}) %copy-start) | copy-done | bytes 524312
  47.1 0.0 copy-start.1
  47.1 0.8 %copy-done.1 = f32[256,512]{1,0:T(8,128)} copy-done((f32[256,512]{1,0:T(8,128)}, f32[256,512]{1,0:T(8,128)S(1)}, u32[]{:S(2)}) %copy-start.1) | copy-done | bytes 524312
  47.9 7.4 %apply.1 = f32[1152,512]{1,0:T(8,128)} custom-call(bf16[4,13,128,256]{3,2,1,0:T(8,128)(2,1)} %prep.1.q_ref, f32[256,512]{1,0:T(8,128)} %copy-done.1, f32[1152,512]{1,0:T(8,128)} %x_ref.1, f32[256,512]{1,0:T(8,128)} %copy-done), custom_call_target="tpu_custom_call" | custom-call | tf_op jit(solution)/shard_map/apply/pallas_call | solution.py:160
Async XLA Ops:
  0.8 14.0 %collective-permute-start = (f32[32,128]{1,0:T(8,128)S(1)}, f32[32,128]{1,0:T(8,128)S(1)}, u32[]{:S(2)}, u32[]{:S(2)}) collective-permute-start(f32[32,128]{1,0:T(8,128)S(1)} %get-tuple-element.7), channel_id=1, source_target_pairs={{0,8},{8,16},{16,24},{1,9},{9,17},{17,25},{2,10},{10,18},{18,26},{... | collective-permute-start | bytes 49160 | tf_op jit(solution)/shard_map/ppermute | solution.py:140
  5.7 9.1 %collective-permute-start.1 = (f32[32,128]{1,0:T(8,128)S(1)}, f32[32,128]{1,0:T(8,128)S(1)}, u32[]{:S(2)}, u32[]{:S(2)}) collective-permute-start(f32[32,128]{1,0:T(8,128)S(1)} %get-tuple-element.8), channel_id=1, source_target_pairs={{8,0},{16,8},{24,16},{9,1},{17,9},{25,17},{10,2},{18,10},{26,18},{... | collective-permute-start | bytes 49160 | tf_op jit(solution)/shard_map/ppermute | solution.py:141
  8.3 38.0 %collective-permute-start.3 = (f32[256,512]{1,0:T(8,128)S(1)}, f32[256,512]{1,0:T(8,128)S(1)}, u32[]{:S(2)}, u32[]{:S(2)}) collective-permute-start(f32[256,512]{1,0:T(8,128)S(1)} %get-tuple-element.5), channel_id=1, source_target_pairs={{8,0},{16,8},{24,16},{9,1},{17,9},{25,17},{10,2},{18,10},{26,18},{... | collective-permute-start | bytes 1572872 | tf_op jit(solution)/shard_map/ppermute | solution.py:143
  9.6 36.7 %collective-permute-start.2 = (f32[256,512]{1,0:T(8,128)S(1)}, f32[256,512]{1,0:T(8,128)S(1)}, u32[]{:S(2)}, u32[]{:S(2)}) collective-permute-start(f32[256,512]{1,0:T(8,128)S(1)} %get-tuple-element.6), channel_id=1, source_target_pairs={{0,8},{8,16},{16,24},{1,9},{9,17},{17,25},{2,10},{10,18},{18,26},{... | collective-permute-start | bytes 1572872 | tf_op jit(solution)/shard_map/ppermute | solution.py:142
  46.3 0.8 %copy-start = (f32[256,512]{1,0:T(8,128)}, f32[256,512]{1,0:T(8,128)S(1)}, u32[]{:S(2)}) copy-start(f32[256,512]{1,0:T(8,128)S(1)} %collective-permute-done.3.below_ref) | copy-start | bytes 1572868
  47.1 0.8 %copy-start.1 = (f32[256,512]{1,0:T(8,128)}, f32[256,512]{1,0:T(8,128)S(1)}, u32[]{:S(2)}) copy-start(f32[256,512]{1,0:T(8,128)S(1)} %collective-permute-done.2.above_ref) | copy-start | bytes 1572868
where the time goes:
time: 56.3 us; the launch traced here: 55.3 us
  Pallas kernels  20.7 us (37%)
  blocking collectives  17.3 us (31%)
  starting transfers between devices  12.7 us (23%)
  local copies, waits for them, and re-layouts  3.67 us (7%)
  other arithmetic  0.97 us (2%)
    all_gather x1, blocking collectives, shards(): everything = lax.all_gather(stored, 'col', axis=0, tiled=True)  17.3 us
    pallas_call x1, Pallas kernels, shards(): pl.pallas_call(functools.partial(prep_kernel, own, own * count), grid=(GR...  13.2 us
    pallas_call x1, Pallas kernels, shards(): pl.pallas_call(functools.partial(apply_kernel, own), grid=(columns // til...  7.4 us
    ppermute x1, starting transfers between devices, shards(): above = lax.ppermute(vectors[rows - HALO:], 'row', forward)  5.21 us
    ppermute x1, starting transfers between devices, shards(): lax.ppermute(reflectors[:, reflectors.shape[1] - width:], 'row', forward)  4.86 us
    unnamed x4, local copies, waits for them, and re-layouts  1.57 us
    ppermute x1, starting transfers between devices, shards(): after = lax.ppermute(reflectors[:, :width], 'row', backward)  1.29 us
    ppermute x1, starting transfers between devices, shards(): below = lax.ppermute(vectors[:HALO], 'row', backward)  1.29 us
  transfers between devices with their start and end apart: 4, of which 0 were waited for; matrix products, arithmetic and copies ran while one was open for 4% of the time, Pallas kernels for 24%

commit v1 on v0

--- a/solution.py
+++ b/solution.py
@@ -36,8 +36,7 @@
     return dot(jnp.concatenate([ah, al], 1), jnp.concatenate([bh, bh], 0)) + dot(ah, bl)
 
 
-def prep_kernel(own, all_windows, refl_ref, q_ref):
-    group = pl.program_id(0)
+def build_group(own, all_windows, group, refl, q_ref):
     first = lax.axis_index("row") * own - SIDE
     size = WIN
     held = own + 2 * SIDE
@@ -53,9 +52,9 @@
     skews, nils, invs, scaled = [], [], [], []
     for pair in range(pairs):
         if (pair + 1) * size <= held * BAND:
-            slab = refl_ref[:, pair * size : (pair + 1) * size]
+            slab = refl[:, pair * size : (pair + 1) * size]
         else:
-            part = refl_ref[:, pair * size : pair * size + BAND]
+            part = refl[:, pair * size : pair * size + BAND]
             slab = jnp.concatenate([part, jnp.zeros_like(part)], 1)
         both = jnp.concatenate([slab, slab], 0)
         both = jnp.where(lead, 1.0, jnp.where(inside, both, 0.0))
@@ -101,8 +100,122 @@
             window = first + k
             weight = ((window >= 0) & (window < usable)).astype(jnp.float32)
             high, low = split(identity - weight * change)
-            q_ref[0, k, :, :size] = high
-            q_ref[0, k, :, size:] = low
+            q_ref[group, k, :, :size] = high
+            q_ref[group, k, :, size:] = low
+
+
+def mixed(a, b, count):
+    total, bit = 0, 1
+    while bit < count:
+        total = total + ((a // bit + b // bit) % 2) * bit
+        bit *= 2
+    return total
+
+
+def gather_kernel(
+    own, rows_axis, cols_axis, refl_ref, head_ref, tail_ref, x_ref,
+    q_ref, above_ref, below_ref,
+    main, left, right, near_send, near_recv, line_send, line_recv, pair_send, pair_recv, own_sem,
+):
+    row, me = lax.axis_index("row"), lax.axis_index("col")
+    chips = cols_axis // 2
+    chip, core = me // 2, me % 2
+    up, down = (row + rows_axis - 1) % rows_axis, (row + 1) % rows_axis
+    other = chip * 2 + 1 - core
+    rows = x_ref.shape[0]
+    mesh_ids = pl.DeviceIdType.MESH
+
+    barrier = pltpu.get_barrier_semaphore()
+    partners = [(row, mixed(chip, i, chips) * 2 + core) for i in range(1, chips)]
+    partners += [(row, other), (up, me), (down, me)]
+    for partner in partners:
+        pl.semaphore_signal(barrier, inc=1, device_id=partner, device_id_type=mesh_ids)
+    pl.semaphore_wait(barrier, len(partners))
+
+    def remote(source, target, send, recv, device):
+        return pltpu.make_async_remote_copy(
+            src_ref=source, dst_ref=target, send_sem=send, recv_sem=recv,
+            device_id=device, device_id_type=mesh_ids,
+        )
+
+    slots = (main, left, right)
+    pending = []
+
+    def share(kind, source):
+        pair = remote(source, slots[kind].at[me], pair_send.at[kind, chip], pair_recv.at[kind, chip], (row, other))
+        pair.start()
+        pending.append(pair)
+        for i in range(1, chips):
+            there = mixed(chip, i, chips)
+            line = remote(source, slots[kind].at[me], line_send.at[kind, there], line_recv.at[kind, chip], (row, there * 2 + core))
+            line.start()
+            pending.append(line)
+
+    near = [
+        remote(tail_ref, left.at[me], near_send.at[0], near_recv.at[0], (down, me)),
+        remote(head_ref, right.at[me], near_send.at[1], near_recv.at[1], (up, me)),
+    ]
+    for copy in near:
+        copy.start()
+    local = pltpu.make_async_copy(refl_ref, main.at[me], own_sem)
+    local.start()
+    share(0, refl_ref)
+    halos = [
+        remote(x_ref.at[pl.ds(rows - HALO, HALO)], above_ref, near_send.at[2], near_recv.at[2], (down, me)),
+        remote(x_ref.at[pl.ds(0, HALO)], below_ref, near_send.at[3], near_recv.at[3], (up, me)),
+    ]
+    for copy in halos:
+        copy.start()
+    for kind, copy in zip((1, 2), near):
+        copy.wait_recv()
+        share(kind, slots[kind].at[me])
+    local.wait()
+
+    def arrived(kind, there, mine, recv):
+        slot = slots[kind].at[there * 2 + (core if mine else 1 - core)]
+        remote(slot, slot, own_sem, recv.at[kind, there], (row, other)).wait_recv()
+
+    share_group = cols_axis // GROUPS
+    chip_group = share_group // 2
+    mine = chip // chip_group
+
+    def members(i):
+        base = mixed(mine, i, GROUPS) * chip_group
+        return [base + mixed(chip % chip_group, j, chip_group) for j in range(chip_group)]
+
+    def forward(i):
+        for j, there in enumerate(members(i)):
+            if i == 0 and j == 0:
+                continue
+            for kind in range(3):
+                arrived(kind, there, True, line_recv)
+                slot = slots[kind].at[there * 2 + core]
+                copy = remote(slot, slot, pair_send.at[kind, there], pair_recv.at[kind, there], (row, other))
+                copy.start()
+                pending.append(copy)
+
+    def build(i):
+        for there in members(i):
+            for kind in range(3):
+                arrived(kind, there, False, pair_recv)
+        group = mixed(mine, i, GROUPS)
+        parts = [slot[pl.ds(group * share_group, share_group)] for slot in (left, main, right)]
+        refl = jnp.concatenate([p.reshape(BAND, p.shape[2]) for p in parts], 1)
+        build_group(own, own * rows_axis, group, refl, q_ref)
+
+    forward(0)
+    build(0)
+    forward(1)
+    for i in range(1, GROUPS):
+        if i + 1 < GROUPS:
+            forward(i + 1)
+        build(i)
+    for copy in halos:
+        copy.wait()
+    for copy in near:
+        copy.wait_send()
+    for copy in pending:
+        copy.wait_send()
 
 
 def apply_kernel(own, q_ref, above_ref, x_ref, below_ref, out_ref, work_ref):
@@ -133,29 +246,34 @@
 def shards(vectors, reflectors):
     rows, columns = vectors.shape
     own = rows // WIN
-    count = lax.axis_size("row")
-    forward = [(i, i + 1) for i in range(count - 1)]
-    backward = [(i + 1, i) for i in range(count - 1)]
+    rows_axis, cols_axis = lax.axis_size("row"), lax.axis_size("col")
     width = SIDE * BAND
-    before = lax.ppermute(reflectors[:, reflectors.shape[1] - width :], "row", forward)
-    after = lax.ppermute(reflectors[:, :width], "row", backward)
-    above = lax.ppermute(vectors[rows - HALO :], "row", forward)
-    below = lax.ppermute(vectors[:HALO], "row", backward)
-    stored = jnp.concatenate([before, reflectors, after], 1)
-    everything = lax.all_gather(stored, "col", axis=0, tiled=True)
-
+    slots, stored = reflectors.shape
+    head, tail = reflectors[:, :width], reflectors[:, stored - width :]
     held = own + 2 * SIDE
-    q = pl.pallas_call(
-        functools.partial(prep_kernel, own, own * count),
-        grid=(GROUPS,),
-        in_specs=[pl.BlockSpec((BAND, held * BAND), lambda g: (g, 0))],
-        out_specs=pl.BlockSpec((1, held, WIN, 2 * WIN), lambda g: (g, 0, 0, 0)),
-        out_shape=jax.ShapeDtypeStruct((GROUPS, held, WIN, 2 * WIN), jnp.bfloat16),
-        cost_estimate=pl.CostEstimate(
-            flops=GROUPS * held * 60 * WIN**3, bytes_accessed=2**22, transcendentals=0
-        ),
-        name="prep",
-    )(everything)
+    anywhere = pl.BlockSpec(memory_space=pl.ANY)
+    halo = jax.ShapeDtypeStruct((HALO, columns), vectors.dtype)
+    dma = pltpu.SemaphoreType.DMA
+    q, above, below = pl.pallas_call(
+        functools.partial(gather_kernel, own, rows_axis, cols_axis),
+        in_specs=[anywhere] * 4,
+        out_specs=[pl.BlockSpec(memory_space=pltpu.VMEM), anywhere, anywhere],
+        out_shape=[jax.ShapeDtypeStruct((GROUPS, held, WIN, 2 * WIN), jnp.bfloat16), halo, halo],
+        scratch_shapes=[
+            pltpu.VMEM((cols_axis, slots, stored), jnp.float32),
+            pltpu.VMEM((cols_axis, slots, width), jnp.float32),
+            pltpu.VMEM((cols_axis, slots, width), jnp.float32),
+            dma((4,)),
+            dma((4,)),
+            dma((3, cols_axis // 2)),
+            dma((3, cols_axis // 2)),
+            dma((3, cols_axis // 2)),
+            dma((3, cols_axis // 2)),
+            dma,
+        ],
+        compiler_params=pltpu.CompilerParams(collective_id=0, has_side_effects=True),
+        name="gather",
+    )(reflectors, head, tail, vectors)
     tile = min(columns, 256)
     return pl.pallas_call(
         functools.partial(apply_kernel, own),

time: 56.3 us -> 41.8 us (0.74); the launches traced: 55.3 us -> 41.6 us
  Pallas kernels: 20.7 us -> 40.2 us
  blocking collectives: 17.3 us -> 0 us
  starting transfers between devices: 12.7 us -> 0 us
  local copies, waits for them, and re-layouts: 3.67 us -> 1.44 us
  other arithmetic: 0.97 us -> 0 us
    pallas_call x1, Pallas kernels: 13.2 us -> 32.7 us  [shards(): pl.pallas_call(functools.partial(gather_kernel, own, rows_axis, cols_axis...]
    all_gather x1 -> x0, blocking collectives: 17.3 us -> none  [shards(): everything = lax.all_gather(stored, 'col', axis=0, tiled=True)]
    ppermute x4 -> x0, starting transfers between devices: 12.7 us -> none  [the longest x1 5.21 us: shards(): above = lax.ppermute(vectors[rows - HALO:], 'row', forward)]
    unnamed x4 -> x0, local copies, waits for them, and re-layouts: 1.57 us -> none
    concatenate x1 -> x0, other arithmetic: 0.97 us -> none  [shards(): stored = jnp.concatenate([before, reflectors, after], 1)]
    slice x2 -> x1, local copies, waits for them, and re-layouts: 2.1 us -> 1.44 us  [shards(): head, tail = (reflectors[:, :width], reflectors[:, stored - width:])]
  transfers between devices with their start and end apart: 4 -> 0, of which waited for: 0 -> 0; matrix products, arithmetic and copies ran while one was open for 4% -> 0% of each run, Pallas kernels for 24% -> 0%
where the time goes in v1:
time: 41.8 us; the launch traced here: 41.6 us
  Pallas kernels  40.2 us (96%)
  local copies, waits for them, and re-layouts  1.44 us (3%)
    pallas_call x1, Pallas kernels, shards(): pl.pallas_call(functools.partial(gather_kernel, own, rows_axis, cols_axis...  32.7 us
    pallas_call x1, Pallas kernels, shards(): pl.pallas_call(functools.partial(apply_kernel, own), grid=(columns // til...  7.43 us
    slice x1, local copies, waits for them, and re-layouts, shards(): head, tail = (reflectors[:, :width], reflectors[:, stored - width:])  1.44 us

profile of v1, /device:TPU:0, one launch (start us, length us, event | category | flops | bytes accessed | tf_op | source)
XLA Modules:
  0.0 41.6 jit_solution(1021073324849754351)
XLA Ops:
  0.0 1.4 %fusion = (f32[32,128]{1,0:T(8,128)}, f32[32,128]{1,0:T(8,128)}) fusion(f32[32,576]{1,0:T(8,128)} %refl_ref.1), kind=kLoop, calls=%fused_computation | loop fusion | bytes 65536 | tf_op jit(solution)/shard_map/slice | solution.py:252
  1.4 32.7 %gather.1 = (bf16[4,13,128,256]{3,2,1,0:T(8,128)(2,1)}, f32[256,512]{1,0:T(8,128)}, f32[256,512]{1,0:T(8,128)}) custom-call(f32[32,576]{1,0:T(8,128)} %refl_ref.1, f32[32,128]{1,0:T(8,128)} %get-tuple-element.12.head_ref, f32[32,128]{1,0:T(8,128)} %get-tuple-element.11.tail_ref, f32[1152,512]{1,0:T(8,128)} %x_ref.3), custom_call_target="tpu_custom_call" | custom-call | tf_op jit(solution)/shard_map/gather/pallas_call | solution.py:257
  34.2 7.4 %apply.1 = f32[1152,512]{1,0:T(8,128)} custom-call(bf16[4,13,128,256]{3,2,1,0:T(8,128)(2,1)} %get-tuple-element.8.q_ref, f32[256,512]{1,0:T(8,128)} %get-tuple-element.9.above_ref, f32[1152,512]{1,0:T(8,128)} %x_ref.3, f32[256,512]{1,0:T(8,128)} %get-tuple-element.10.below_ref), custom_call_target="tpu_custom_call" | custom-call | tf_op jit(solution)/shard_map/apply/pallas_call | solution.py:278

commit v2 on v1

--- a/solution.py
+++ b/solution.py
@@ -112,10 +112,24 @@
     return total
 
 
+def apply_windows(windows, q_ref, work):
+    columns = work.shape[1]
+    tile = min(columns, 256)
+
+    def one_tile(step, carry):
+        cols = pl.ds(pl.multiple_of(step * tile, tile), tile)
+        for group, k, at in windows:
+            xh, xl = split(work[at : at + WIN, cols])
+            q = q_ref[group, k]
+            work[at : at + WIN, cols] = dot(q, jnp.concatenate([xh, xh], 0)) + dot(q[:, :WIN], xl)
+        return carry
+
+    lax.fori_loop(0, columns // tile, one_tile, 0)
+
+
 def gather_kernel(
-    own, rows_axis, cols_axis, refl_ref, head_ref, tail_ref, x_ref,
-    q_ref, above_ref, below_ref,
-    main, left, right, near_send, near_recv, line_send, line_recv, pair_send, pair_recv, own_sem,
+    own, rows_axis, cols_axis, refl_ref, head_ref, tail_ref, x_ref, out_ref,
+    q_ref, work, main, left, right, near_send, near_recv, line_send, line_recv, pair_send, pair_recv, own_sem, x_sem, out_sem,
 ):
     row, me = lax.axis_index("row"), lax.axis_index("col")
     chips = cols_axis // 2
@@ -157,15 +171,17 @@
     ]
     for copy in near:
         copy.start()
+    halos = [
+        remote(x_ref.at[pl.ds(rows - HALO, HALO)], work.at[pl.ds(0, HALO)], near_send.at[2], near_recv.at[2], (down, me)),
+        remote(x_ref.at[pl.ds(0, HALO)], work.at[pl.ds(HALO + rows, HALO)], near_send.at[3], near_recv.at[3], (up, me)),
+    ]
+    for copy in halos:
+        copy.start()
+    fill = pltpu.make_async_copy(x_ref, work.at[pl.ds(HALO, rows)], x_sem)
     local = pltpu.make_async_copy(refl_ref, main.at[me], own_sem)
     local.start()
     share(0, refl_ref)
-    halos = [
-        remote(x_ref.at[pl.ds(rows - HALO, HALO)], above_ref, near_send.at[2], near_recv.at[2], (down, me)),
-        remote(x_ref.at[pl.ds(0, HALO)], below_ref, near_send.at[3], near_recv.at[3], (up, me)),
-    ]
-    for copy in halos:
-        copy.start()
+    fill.start()
     for kind, copy in zip((1, 2), near):
         copy.wait_recv()
         share(kind, slots[kind].at[me])
@@ -210,37 +226,38 @@
         if i + 1 < GROUPS:
             forward(i + 1)
         build(i)
+    inner, outer = [], []
+    for group in range(GROUPS):
+        start, count = group_range(group, own)
+        for k in range(start, start + count):
+            at = BAND * (group % 2) + WIN * k
+            free = at >= HALO + BAND * group and at + WIN <= HALO + rows - BAND * group
+            (inner if free else outer).append((group, k, at))
+
+    fill.wait()
+    apply_windows(inner, q_ref, work)
+    margin = BAND * (GROUPS - 1)
+
+    def result(first, size, at):
+        return pltpu.make_async_copy(
+            work.at[pl.ds(HALO + first, size)], out_ref.at[pl.ds(first, size)], out_sem.at[at]
+        )
+
+    results = [result(margin, rows - 2 * margin, 0), result(0, margin, 1), result(rows - margin, margin, 2)]
+    results[0].start()
     for copy in halos:
+        copy.wait_recv()
+    apply_windows(outer, q_ref, work)
+    for copy in results[1:]:
+        copy.start()
+    for copy in results:
         copy.wait()
+    for copy in halos:
+        copy.wait_send()
     for copy in near:
         copy.wait_send()
     for copy in pending:
         copy.wait_send()
-
-
-def apply_kernel(own, q_ref, above_ref, x_ref, below_ref, out_ref, work_ref):
-    rows = x_ref.shape[0]
-    for group in range(GROUPS):
-        start, count = group_range(group, own)
-        for k in range(start, start + count):
-            at = BAND * (group % 2) + WIN * k
-            if group == 0:
-                if at < HALO:
-                    block = above_ref[at : at + WIN, :]
-                elif at < HALO + rows:
-                    block = x_ref[at - HALO : at - HALO + WIN, :]
-                else:
-                    block = below_ref[at - HALO - rows : at - HALO - rows + WIN, :]
-            else:
-                block = work_ref[at : at + WIN, :]
-            xh, xl = split(block)
-            q = q_ref[group, k]
-            new = dot(q, jnp.concatenate([xh, xh], 0)) + dot(q[:, :WIN], xl)
-            if group < GROUPS - 1:
-                work_ref[at : at + WIN, :] = new
-            else:
-                low, high = max(at, HALO), min(at + WIN, HALO + rows)
-                out_ref[low - HALO : high - HALO, :] = new[low - at : high - at, :]
 
 
 def shards(vectors, reflectors):
@@ -252,14 +269,15 @@
     head, tail = reflectors[:, :width], reflectors[:, stored - width :]
     held = own + 2 * SIDE
     anywhere = pl.BlockSpec(memory_space=pl.ANY)
-    halo = jax.ShapeDtypeStruct((HALO, columns), vectors.dtype)
     dma = pltpu.SemaphoreType.DMA
-    q, above, below = pl.pallas_call(
+    return pl.pallas_call(
         functools.partial(gather_kernel, own, rows_axis, cols_axis),
         in_specs=[anywhere] * 4,
-        out_specs=[pl.BlockSpec(memory_space=pltpu.VMEM), anywhere, anywhere],
-        out_shape=[jax.ShapeDtypeStruct((GROUPS, held, WIN, 2 * WIN), jnp.bfloat16), halo, halo],
+        out_specs=anywhere,
+        out_shape=jax.ShapeDtypeStruct(vectors.shape, vectors.dtype),
         scratch_shapes=[
+            pltpu.VMEM((GROUPS, held, WIN, 2 * WIN), jnp.bfloat16),
+            pltpu.VMEM((rows + 2 * HALO, columns), jnp.float32),
             pltpu.VMEM((cols_axis, slots, stored), jnp.float32),
             pltpu.VMEM((cols_axis, slots, width), jnp.float32),
             pltpu.VMEM((cols_axis, slots, width), jnp.float32),
@@ -270,25 +288,12 @@
             dma((3, cols_axis // 2)),
             dma((3, cols_axis // 2)),
             dma,
+            dma,
+            dma((3,)),
         ],
         compiler_params=pltpu.CompilerParams(collective_id=0, has_side_effects=True),
         name="gather",
     )(reflectors, head, tail, vectors)
-    tile = min(columns, 256)
-    return pl.pallas_call(
-        functools.partial(apply_kernel, own),
-        grid=(columns // tile,),
-        in_specs=[
-            pl.BlockSpec(q.shape, lambda c: (0, 0, 0, 0)),
-            pl.BlockSpec((HALO, tile), lambda c: (0, c)),
-            pl.BlockSpec((rows, tile), lambda c: (0, c)),
-            pl.BlockSpec((HALO, tile), lambda c: (0, c)),
-        ],
-        out_specs=pl.BlockSpec((rows, tile), lambda c: (0, c)),
-        out_shape=jax.ShapeDtypeStruct(vectors.shape, vectors.dtype),
-        scratch_shapes=[pltpu.VMEM((rows + 2 * HALO, tile), jnp.float32)],
-        name="apply",
-    )(q, above, vectors, below)
 
 
 def solution(mesh):

time: 41.8 us -> 38.7 us (0.926)
  Pallas kernels: 40.2 us -> 33.8 us
  local copies, waits for them, and re-layouts: 1.44 us -> 4.71 us
    pallas_call x1 -> x0, Pallas kernels: 7.43 us -> none  [shards(): pl.pallas_call(functools.partial(apply_kernel, own), grid=(columns // til...]
    unnamed x0 -> x1, local copies, waits for them, and re-layouts: none -> 3.27 us
    pallas_call x1, Pallas kernels: 32.7 us -> 33.8 us  [shards(): pl.pallas_call(functools.partial(gather_kernel, own, rows_axis, cols_axis...]
where the time goes in v2:
time: 38.7 us; the launch traced here: 38.5 us
  Pallas kernels  33.8 us (87%)
  local copies, waits for them, and re-layouts  4.71 us (12%)
    pallas_call x1, Pallas kernels, shards(): pl.pallas_call(functools.partial(gather_kernel, own, rows_axis, cols_axis...  33.8 us
    unnamed x1, local copies, waits for them, and re-layouts  3.27 us
    slice x1, local copies, waits for them, and re-layouts, shards(): head, tail = (reflectors[:, :width], reflectors[:, stored - width:])  1.44 us

profile of v2, /device:TPU:0, one launch (start us, length us, event | category | flops | bytes accessed | tf_op | source)
XLA Modules:
  0.0 38.5 jit_solution(49727987929359050)
XLA Ops:
  0.0 1.4 %fusion = (f32[32,128]{1,0:T(8,128)}, f32[32,128]{1,0:T(8,128)}) fusion(f32[32,576]{1,0:T(8,128)} %refl_ref.1), kind=kLoop, calls=%fused_computation | loop fusion | bytes 65536 | tf_op jit(solution)/shard_map/slice | solution.py:269
  1.4 33.8 %gather.1 = f32[1152,512]{1,0:T(8,128)} custom-call(f32[32,576]{1,0:T(8,128)} %refl_ref.1, f32[32,128]{1,0:T(8,128)} %get-tuple-element.6.head_ref, f32[32,128]{1,0:T(8,128)} %get-tuple-element.5.tail_ref, f32[1152,512]{1,0:T(8,128)} %x_ref.1), custom_call_target="tpu_custom_call" | custom-call | tf_op jit(solution)/shard_map/gather/pallas_call | solution.py:273
  35.2 3.3 %copy.4 = f32[1152,512]{1,0:T(8,128)} copy(f32[1152,512]{1,0:T(8,128)} %gather.1) | data formatting | bytes 4718592

commit v3 on v2

--- a/solution.py
+++ b/solution.py
@@ -128,7 +128,7 @@
 
 
 def gather_kernel(
-    own, rows_axis, cols_axis, refl_ref, head_ref, tail_ref, x_ref, out_ref,
+    own, rows_axis, cols_axis, refl_ref, tail_ref, x_ref, out_ref,
     q_ref, work, main, left, right, near_send, near_recv, line_send, line_recv, pair_send, pair_recv, own_sem, x_sem, out_sem,
 ):
     row, me = lax.axis_index("row"), lax.axis_index("col")
@@ -167,14 +167,18 @@
 
     near = [
         remote(tail_ref, left.at[me], near_send.at[0], near_recv.at[0], (down, me)),
-        remote(head_ref, right.at[me], near_send.at[1], near_recv.at[1], (up, me)),
+        remote(refl_ref.at[:, pl.ds(0, right.shape[2])], right.at[me], near_send.at[1], near_recv.at[1], (up, me)),
     ]
     for copy in near:
         copy.start()
-    halos = [
-        remote(x_ref.at[pl.ds(rows - HALO, HALO)], work.at[pl.ds(0, HALO)], near_send.at[2], near_recv.at[2], (down, me)),
-        remote(x_ref.at[pl.ds(0, HALO)], work.at[pl.ds(HALO + rows, HALO)], near_send.at[3], near_recv.at[3], (up, me)),
-    ]
+    half = HALO // 2
+    halos = []
+    for part, offset in enumerate((half, 0)):
+        above = (x_ref.at[pl.ds(rows - HALO + offset, half)], work.at[pl.ds(offset, half)])
+        below = (x_ref.at[pl.ds(half - offset, half)], work.at[pl.ds(HALO + rows + half - offset, half)])
+        at = 2 + 2 * part
+        halos.append(remote(*above, near_send.at[at], near_recv.at[at], (down, me)))
+        halos.append(remote(*below, near_send.at[at + 1], near_recv.at[at + 1], (up, me)))
     for copy in halos:
         copy.start()
     fill = pltpu.make_async_copy(x_ref, work.at[pl.ds(HALO, rows)], x_sem)
@@ -226,30 +230,41 @@
         if i + 1 < GROUPS:
             forward(i + 1)
         build(i)
-    inner, outer = [], []
+    parts = ([], [], [])
     for group in range(GROUPS):
         start, count = group_range(group, own)
         for k in range(start, start + count):
             at = BAND * (group % 2) + WIN * k
-            free = at >= HALO + BAND * group and at + WIN <= HALO + rows - BAND * group
-            (inner if free else outer).append((group, k, at))
+            for part, reach in enumerate((0, half, HALO)):
+                low = HALO - reach + BAND * group
+                if at >= low and at + WIN <= 2 * HALO + rows - low:
+                    parts[part].append((group, k, at))
+                    break
 
     fill.wait()
-    apply_windows(inner, q_ref, work)
+    apply_windows(parts[0], q_ref, work)
     margin = BAND * (GROUPS - 1)
+    nearer = margin - half
 
     def result(first, size, at):
         return pltpu.make_async_copy(
             work.at[pl.ds(HALO + first, size)], out_ref.at[pl.ds(first, size)], out_sem.at[at]
         )
 
-    results = [result(margin, rows - 2 * margin, 0), result(0, margin, 1), result(rows - margin, margin, 2)]
+    results = [
+        result(margin, rows - 2 * margin, 0),
+        result(nearer, half, 1),
+        result(rows - margin, half, 2),
+        result(0, nearer, 3),
+        result(rows - nearer, nearer, 4),
+    ]
     results[0].start()
-    for copy in halos:
-        copy.wait_recv()
-    apply_windows(outer, q_ref, work)
-    for copy in results[1:]:
-        copy.start()
+    for part in range(2):
+        for copy in halos[2 * part : 2 * part + 2]:
+            copy.wait_recv()
+        apply_windows(parts[1 + part], q_ref, work)
+        for copy in results[1 + 2 * part : 3 + 2 * part]:
+            copy.start()
     for copy in results:
         copy.wait()
     for copy in halos:
@@ -266,13 +281,13 @@
     rows_axis, cols_axis = lax.axis_size("row"), lax.axis_size("col")
     width = SIDE * BAND
     slots, stored = reflectors.shape
-    head, tail = reflectors[:, :width], reflectors[:, stored - width :]
+    tail = reflectors[:, stored - width :]
     held = own + 2 * SIDE
     anywhere = pl.BlockSpec(memory_space=pl.ANY)
     dma = pltpu.SemaphoreType.DMA
     return pl.pallas_call(
         functools.partial(gather_kernel, own, rows_axis, cols_axis),
-        in_specs=[anywhere] * 4,
+        in_specs=[pl.BlockSpec(memory_space=pltpu.HBM)] * 3,
         out_specs=anywhere,
         out_shape=jax.ShapeDtypeStruct(vectors.shape, vectors.dtype),
         scratch_shapes=[
@@ -281,19 +296,19 @@
             pltpu.VMEM((cols_axis, slots, stored), jnp.float32),
             pltpu.VMEM((cols_axis, slots, width), jnp.float32),
             pltpu.VMEM((cols_axis, slots, width), jnp.float32),
-            dma((4,)),
-            dma((4,)),
+            dma((6,)),
+            dma((6,)),
             dma((3, cols_axis // 2)),
             dma((3, cols_axis // 2)),
             dma((3, cols_axis // 2)),
             dma((3, cols_axis // 2)),
             dma,
             dma,
-            dma((3,)),
+            dma((5,)),
         ],
-        compiler_params=pltpu.CompilerParams(collective_id=0, has_side_effects=True),
+        compiler_params=pltpu.CompilerParams(collective_id=0, has_side_effects=True, vmem_limit_bytes=24 * 2**20),
         name="gather",
-    )(reflectors, head, tail, vectors)
+    )(reflectors, tail, vectors)
 
 
 def solution(mesh):

time: 38.7 us -> 37.9 us (0.979)
  Pallas kernels: 33.8 us -> 32.8 us
    pallas_call x1, Pallas kernels: 33.8 us -> 32.8 us  [shards(): pl.pallas_call(functools.partial(gather_kernel, own, rows_axis, cols_axis...]
    unnamed x1 -> x5, local copies, waits for them, and re-layouts: 3.27 us -> 3.96 us
    slice x1, local copies, waits for them, and re-layouts: 1.44 us -> 0.83 us  [shards(): tail = reflectors[:, stored - width:]]
where the time goes in v3:
time: 37.9 us; the launch traced here: 37.6 us
  Pallas kernels  32.8 us (87%)
  local copies, waits for them, and re-layouts  4.79 us (13%)
    pallas_call x1, Pallas kernels, shards(): pl.pallas_call(functools.partial(gather_kernel, own, rows_axis, cols_axis...  32.8 us
    unnamed x5, local copies, waits for them, and re-layouts  3.96 us
    slice x1, local copies, waits for them, and re-layouts, shards(): tail = reflectors[:, stored - width:]  0.83 us

profile of v3, /device:TPU:0, one launch (start us, length us, event | category | flops | bytes accessed | tf_op | source)
XLA Modules:
  0.0 37.6 jit_solution(16843717237126223001)
XLA Ops:
  0.0 0.8 %slice.3.tail_ref = f32[32,128]{1,0:T(8,128)S(1)} slice(f32[32,576]{1,0:T(8,128)} %refl_ref.1), slice={[0:32], [448:576]} | slice | bytes 32768 | tf_op jit(solution)/shard_map/slice | solution.py:284
  0.8 0.0 copy-start
  0.8 1.7 %copy-done = f32[1152,512]{1,0:T(8,128)S(1)} copy-done((f32[1152,512]{1,0:T(8,128)S(1)}, f32[1152,512]{1,0:T(8,128)}, u32[]{:S(2)}) %copy-start) | copy-done | bytes 2359320
  2.5 0.0 copy-start.1
  2.5 0.9 %copy-done.1 = f32[32,576]{1,0:T(8,128)S(1)} copy-done((f32[32,576]{1,0:T(8,128)S(1)}, f32[32,576]{1,0:T(8,128)}, u32[]{:S(2)}) %copy-start.1) | copy-done | bytes 73752
  3.4 32.8 %gather.1 = f32[1152,512]{1,0:T(8,128)S(1)} custom-call(f32[32,576]{1,0:T(8,128)S(1)} %copy-done.1, f32[32,128]{1,0:T(8,128)S(1)} %slice.3.tail_ref, f32[1152,512]{1,0:T(8,128)S(1)} %copy-done), custom_call_target="tpu_custom_call" | custom-call | tf_op jit(solution)/shard_map/gather/pallas_call | solution.py:288
  36.2 1.4 %copy.4 = f32[1152,512]{1,0:T(8,128)} copy(f32[1152,512]{1,0:T(8,128)S(1)} %gather.1) | data formatting | bytes 4718592
Async XLA Ops:
  0.8 1.7 %copy-start = (f32[1152,512]{1,0:T(8,128)S(1)}, f32[1152,512]{1,0:T(8,128)}, u32[]{:S(2)}) copy-start(f32[1152,512]{1,0:T(8,128)} %x_ref.1) | copy-start | bytes 7077892
  2.5 0.9 %copy-start.1 = (f32[32,576]{1,0:T(8,128)S(1)}, f32[32,576]{1,0:T(8,128)}, u32[]{:S(2)}) copy-start(f32[32,576]{1,0:T(8,128)} %refl_ref.1) | copy-start | bytes 221188

commit v4 on v3

--- a/solution.py
+++ b/solution.py
@@ -306,7 +306,7 @@
             dma,
             dma((5,)),
         ],
-        compiler_params=pltpu.CompilerParams(collective_id=0, has_side_effects=True, vmem_limit_bytes=24 * 2**20),
+        compiler_params=pltpu.CompilerParams(collective_id=0, has_side_effects=True, vmem_limit_bytes=50 * 2**20),
         name="gather",
     )(reflectors, tail, vectors)
 

time: 37.9 us -> 36.2 us (0.955)
  local copies, waits for them, and re-layouts: 4.79 us -> 3.12 us
    unnamed x5 -> x3, local copies, waits for them, and re-layouts: 3.96 us -> 2.3 us
where the time goes in v4:
time: 36.2 us; the launch traced here: 36 us
  Pallas kernels  32.8 us (91%)
  local copies, waits for them, and re-layouts  3.12 us (9%)
    pallas_call x1, Pallas kernels, shards(): pl.pallas_call(functools.partial(gather_kernel, own, rows_axis, cols_axis...  32.8 us
    unnamed x3, local copies, waits for them, and re-layouts  2.3 us
    slice x1, local copies, waits for them, and re-layouts, shards(): tail = reflectors[:, stored - width:]  0.83 us

profile of v4, /device:TPU:0, one launch (start us, length us, event | category | flops | bytes accessed | tf_op | source)
XLA Modules:
  0.0 36.0 jit_solution(2358898325929740215)
XLA Ops:
  0.0 0.8 %slice.3.tail_ref = f32[32,128]{1,0:T(8,128)S(1)} slice(f32[32,576]{1,0:T(8,128)} %refl_ref.1), slice={[0:32], [448:576]} | slice | bytes 32768 | tf_op jit(solution)/shard_map/slice | solution.py:284
  0.8 0.0 copy-start
  0.8 0.9 %copy-done = f32[32,576]{1,0:T(8,128)S(1)} copy-done((f32[32,576]{1,0:T(8,128)S(1)}, f32[32,576]{1,0:T(8,128)}, u32[]{:S(2)}) %copy-start) | copy-done | bytes 73752
  1.7 32.8 %gather.1 = f32[1152,512]{1,0:T(8,128)S(1)} custom-call(f32[32,576]{1,0:T(8,128)S(1)} %copy-done, f32[32,128]{1,0:T(8,128)S(1)} %slice.3.tail_ref, f32[1152,512]{1,0:T(8,128)} %x_ref.1), custom_call_target="tpu_custom_call" | custom-call | tf_op jit(solution)/shard_map/gather/pallas_call | solution.py:288
  34.6 1.4 %copy.4 = f32[1152,512]{1,0:T(8,128)} copy(f32[1152,512]{1,0:T(8,128)S(1)} %gather.1) | data formatting | bytes 4718592
Async XLA Ops:
  0.8 0.9 %copy-start = (f32[32,576]{1,0:T(8,128)S(1)}, f32[32,576]{1,0:T(8,128)}, u32[]{:S(2)}) copy-start(f32[32,576]{1,0:T(8,128)} %refl_ref.1) | copy-start | bytes 221188
